TPU v7x, 128 devices: a whole 4x4x4 slice. The times are simulated.
128 devices in a mesh: tile: 32 (over y, z, core), row: 4 (over x).
Axes of the slice: x: 4, y: 4, z: 4, core: 2. Of those that a mesh axis runs over, the one named last changes fastest.
Arguments:
- cam_disp: bfloat16 [4, 32, 4, 2, 256, 512], P('row', 'tile')
- footprint: int32 [4, 32, 2, 2], P('row', 'tile'), may hold values from 0 to 15, as said below
- stencil: int32 [4, 32, 2, 2, 2, 256], P('row', 'tile'), may hold values from 0 to 12
- frac: float32 [4, 32, 2, 2, 2, 256], P('row', 'tile'), may hold values from 0 to 1
- coef: float32 [4, 32, 2, 3, 4, 256], P('row', 'tile'), may hold values from -3 to 3
Outputs:
- velocity: bfloat16 [4, 32, 2, 3, 256, 512], P('row', 'tile')
- rfactor: float32 [512, 512], replicated
Inputs may be any that keep to these rules, and one draw needn't show every extreme that they name: `footprint`: for each device, the camera tiles named for camera 0 all lie in one row group and are distinct; those for camera 1 lie in other row groups. So a device needs at most 2 distinct camera tiles from any one row group, and exactly 2 from one of them.
All inputs are finite; a program needn't handle non-finite values.
Results may differ from a plain program's by a relative error of at most 0.0015.
The roundings to bfloat16 on the way count: a program that leaves them out, or rounds other values in their place, can miss the bound.
Values may be sent and summed in bfloat16 or wider, within the bound.
No kernel may reach another device: no remote copies, remote signals or barrier semaphores. Data moves between devices by JAX's collectives and lax.ppermute only.
A program may use at most 512 MiB of HBM per device.

v0:
```python
import jax
import jax.numpy as jnp
from jax import lax
from jax.sharding import PartitionSpec as P

TILE_SIDE = 16


def catmull(t):
    k0 = ((-0.5 * t + 1.0) * t - 0.5) * t
    k1 = (1.5 * t - 2.5) * t * t + 1.0
    k2 = ((-1.5 * t + 2.0) * t + 0.5) * t
    k3 = (0.5 * t - 0.5) * t * t
    return (k0, k1, k2, k3)


def axis_weights(base, fraction, side):
    positions = jnp.arange(side, dtype=jnp.int32)
    weights = catmull(fraction)
    total = jnp.zeros(base.shape + (side,), jnp.float32)
    for shift in range(4):
        total = total + weights[shift][..., None] * (positions == base[..., None] + shift).astype(
            jnp.float32
        )
    return total


def local(cam_disp, footprint, stencil, frac, coef):
    cam_count = cam_disp.shape[2]
    pix = cam_disp.shape[4]
    snaps = cam_disp.shape[5]
    world = footprint.shape[2]
    cells = coef.shape[-1]
    groups = lax.axis_size("row")
    tiles = cam_disp.reshape(cam_count, 2, pix, snaps)
    ids = footprint.reshape(world * 2)
    pool = lax.all_gather(tiles, "row", axis=0, tiled=True)
    picked = jnp.take(pool, ids, axis=0)
    sten = stencil.reshape(world * 2, 2, cells)
    fraction = frac.reshape(world * 2, 2, cells)
    row_weights = axis_weights(sten[:, 0], fraction[:, 0], TILE_SIDE)
    col_weights = axis_weights(sten[:, 1], fraction[:, 1], TILE_SIDE)
    mats = (
        (row_weights[:, :, :, None] * col_weights[:, :, None, :])
        .reshape(world * 2, cells, pix)
        .astype(jnp.bfloat16)
    )
    interp = jnp.einsum("pqx,pjxs->pjqs", mats, picked, preferred_element_type=jnp.float32)
    interp = interp.reshape(world, 4, cells, snaps)
    weights_coef = coef.reshape(world, 3, 4, cells)
    total = jnp.zeros((world, 3, cells, snaps), jnp.float32)
    for inner in range(4):
        total = total + weights_coef[:, :, inner, :, None] * interp[:, None, inner]
    velocity = total.astype(jnp.bfloat16)
    rows = velocity.reshape(world * 3 * cells, snaps)
    total_rows = groups * lax.axis_size("tile") * world * 3 * cells
    gram_local = lax.dot_general(
        rows, rows, (((0,), (0,)), ((), ())), preferred_element_type=jnp.float32
    ) / jnp.float32(total_rows)
    gram = lax.psum(gram_local, ("tile", "row"))
    rfactor = jnp.linalg.cholesky(gram).T
    return (velocity.reshape(1, 1, world, 3, cells, snaps), rfactor)


def solution(mesh):
    in_specs = (
        P("row", "tile", None, None, None, None),
        P("row", "tile", None, None),
        P("row", "tile", None, None, None, None),
        P("row", "tile", None, None, None, None),
        P("row", "tile", None, None, None, None),
    )
    out_specs = (P("row", "tile", None, None, None, None), P())
    return jax.shard_map(local, mesh=mesh, in_specs=in_specs, out_specs=out_specs, check_vma=False)
```

profile of v0, /device:TPU:1, one launch (start us, length us, event | category | flops | bytes accessed | tf_op | source)
XLA Modules:
  0.0 350.8 jit_solution(17667153879769481018)
XLA Ops:
  7.2 0.0 all-gather.3.cloned.1.call-start
  7.2 0.7 all-gather.3.cloned.1.call-update
  7.9 0.0 all-reduce.3.cloned.1.call-start
  7.9 0.8 reshape.323
  8.7 0.8 reshape.321
  9.5 0.9 fusion.37
  10.5 0.8 fusion.38
  11.3 0.8 fusion.39
  12.2 0.1 multiply_convert_fusion
  12.3 83.4 %all-gather.3.cloned.1.call-done = bf16[1,1,16,2,256,512]{5,4,3,1,0,2:T(8,128)(2,1)} async-done(((bf16[1,1,4,2,256,512]{5,4,3,1,0,2:T(8,128)(2,1)}), bf16[1,1,16,2,256,512]{5,4,3,1,0,2:T(8,128)(2,1)}) %all-gather.3.cloned.1.call-update) | async-done | bytes 8388624 | tf_op jit(solution)/shard_map/all_gather | solution.py:37
  95.7 4.1 %gather_fusion = bf16[4,2,256,512]{3,2,1,0:T(8,128)(2,1)S(1)} fusion(bf16[16,2,256,512]{3,2,1,0:T(8,128)(2,1)} %bitcast.124, s32[1024]{0:T(1024)S(1)} %pad_clamp_fusion), kind=kCustom, calls=%fused_computation | custom fusion | bytes 4194320 | tf_op jit(solution)/shard_map/jit(_take)/gather | solution.py:38
  99.8 1.0 fusion
  100.8 0.4 slice_bitcast_fusion.3
  101.2 0.0 copy-start
  101.3 0.0 copy-start.1
  101.3 0.9 copy-done
  102.2 0.3 copy-done.1
  102.6 3.4 fusion.13
  105.9 0.0 all-reduce.3.cloned.1.call-update
  106.0 0.3 copy.49
  106.3 0.3 copy.52
  106.6 1.6 copy.55
  108.2 2.5 copy.58
  110.7 2.9 add_convert_fusion.1
  113.6 141.9 %all-reduce.3.cloned.1.call-done = f32[512,512]{0,1:T(8,128)} async-done(((f32[512,512]{0,1:T(8,128)}), f32[512,512]{0,1:T(8,128)}) %all-reduce.3.cloned.1.call-update) | async-done | bytes 1048592 | tf_op jit(solution)/shard_map/psum | solution.py:60
  255.6 1.6 copy.65
  257.1 1.4 fusion.14
  258.6 11.7 %cholesky.104 = f32[128,128]{1,0:T(8,128)S(1)} custom-call(f32[128,128]{1,0:T(8,128)S(1)} %cholesky.266), custom_call_target="Cholesky" | custom-call | tf_op jit(solution)/shard_map/jit(cholesky)/cholesky | solution.py:61
  270.3 0.6 compare_reduce_fusion.3
  271.0 9.8 %custom-call.27 = f32[1,128,128]{1,2,0:T(8,128)S(1)} custom-call(f32[1,128,128]{2,1,0:T(8,128)S(1)} %get-tuple-element.21), custom_call_target="InvertDiagBlocksLowerTriangular" | custom-call | tf_op jit(solution)/shard_map/jit(cholesky)/cholesky | solution.py:61
  280.8 0.1 cholesky.224
  280.9 0.3 constant_dynamic-update-slice_fusion.2
  281.2 0.3 convolution_subtract_fusion
  281.6 11.7 %cholesky.217 = f32[128,128]{1,0:T(8,128)S(1)} custom-call(f32[128,128]{1,0:T(8,128)S(1)} %cholesky.270), custom_call_target="Cholesky" | custom-call | tf_op jit(solution)/shard_map/jit(cholesky)/cholesky | solution.py:61
  293.3 0.7 compare_reduce_fusion.2
  294.1 10.0 %custom-call.28 = f32[1,128,128]{1,2,0:T(8,128)S(1)} custom-call(f32[1,128,128]{2,1,0:T(8,128)S(1)} %get-tuple-element.18), custom_call_target="InvertDiagBlocksLowerTriangular" | custom-call | tf_op jit(solution)/shard_map/jit(cholesky)/cholesky | solution.py:61
  304.1 0.3 convolution_dynamic-update-slice_fusion
  304.3 0.4 convolution_subtract_fusion.1
  304.7 11.7 %cholesky.238 = f32[128,128]{1,0:T(8,128)S(1)} custom-call(f32[128,128]{1,0:T(8,128)S(1)} %cholesky.275), custom_call_target="Cholesky" | custom-call | tf_op jit(solution)/shard_map/jit(cholesky)/cholesky | solution.py:61
  316.5 0.6 compare_reduce_fusion.1
  317.1 9.8 %custom-call.29 = f32[1,128,128]{1,2,0:T(8,128)S(1)} custom-call(f32[1,128,128]{2,1,0:T(8,128)S(1)} %get-tuple-element.15), custom_call_target="InvertDiagBlocksLowerTriangular" | custom-call | tf_op jit(solution)/shard_map/jit(cholesky)/cholesky | solution.py:61
  326.9 0.2 convolution_dynamic-update-slice_fusion.1
  327.1 0.4 convolution_subtract_fusion.2
  327.5 11.7 %cholesky.255 = f32[128,128]{1,0:T(8,128)S(1)} custom-call(f32[128,128]{1,0:T(8,128)S(1)} %convolution_subtract_fusion.2), custom_call_target="Cholesky" | custom-call | tf_op jit(solution)/shard_map/jit(cholesky)/cholesky | solution.py:61
  339.3 0.7 compare_reduce_fusion
  342.5 0.1 select_bitcast_fusion
  342.6 1.3 copy.66
  (21 shorter events, 0.3 us)
Async XLA Ops:
  7.2 88.6 %all-gather.3.cloned.1.call-start = ((), (), s32[]{:S(2)}) async-start(), calls=%async_computation.1 | async-start | bytes 10485760 | tf_op jit(solution)/shard_map/all_gather | solution.py:37
  7.9 247.7 %all-reduce.3.cloned.1.call-start = ((), (), s32[]{:S(2)}) async-start(), calls=%async_computation | async-start | bytes 2097152 | tf_op jit(solution)/shard_map/psum | solution.py:60
  101.2 1.0 copy-start
  101.3 1.3 copy-start.1
Sparse Core Ops, SparseCore 0:
  9.6 86.0 all-gather.2
  106.1 149.4 all-reduce.2
where the time goes:
time: 351 us
  waiting for transfers between devices  226 us (64%)
  other arithmetic  84 us (24%)
  local copies, waits for them, and re-layouts  17.6 us (5%)
  between operations  16.9 us (5%)
  matrix products  6.25 us (2%)
    psum x1, waiting for transfers between devices, local(): gram = lax.psum(gram_local, ('tile', 'row'))  142 us
    all_gather x1, waiting for transfers between devices, local(): pool = lax.all_gather(tiles, 'row', axis=0, tiled=True)  83.4 us
    another operation x15, other arithmetic, local(): rfactor = jnp.linalg.cholesky(gram).T  79.3 us
  transfers between devices with their start and end apart: 2, of which 2 were waited for; matrix products, arithmetic and copies ran while one was open for 3% of the time, Pallas kernels for 0%

commit v1 on v0

v1 whole, which is shorter than its diff:
```python
import functools

import jax
import jax.numpy as jnp
from jax import lax
from jax.experimental import pallas as pl
from jax.experimental.pallas import tpu as pltpu
from jax.sharding import Mesh, PartitionSpec as P

F32 = jnp.float32
BF16 = jnp.bfloat16
TILE_SIDE = 16
CHIPS = ("y", "z", "x")
ANY = pl.BlockSpec(memory_space=pl.ANY)
VM = pl.BlockSpec(memory_space=pltpu.VMEM)


def catmull(t):
    k0 = ((-0.5 * t + 1.0) * t - 0.5) * t
    k1 = (1.5 * t - 2.5) * t * t + 1.0
    k2 = ((-1.5 * t + 2.0) * t + 0.5) * t
    k3 = (0.5 * t - 0.5) * t * t
    return (k0, k1, k2, k3)


def axis_weights(base, fraction, side):
    positions = jnp.arange(side, dtype=jnp.int32)
    weights = catmull(fraction)
    total = jnp.zeros(base.shape + (side,), F32)
    for shift in range(4):
        total = total + weights[shift][..., None] * (positions == base[..., None] + shift).astype(F32)
    return total


def world_kernel(w, pick_ref, cam_ref, r1_ref, r2_ref, r3_ref, mats_ref, coef_ref, *rest):
    if w:
        gin_ref, _, vel_ref, gram_ref, tiles, interp, sem = rest
    else:
        vel_ref, gram_ref, tiles, interp, sem = rest
    cells, snaps = vel_ref.shape[2], vel_ref.shape[3]
    for c in range(2):
        dist = pick_ref[2 * (2 * w + c)]
        index = pick_ref[2 * (2 * w + c) + 1]

        @pl.when(dist == 0)
        def _():
            pltpu.make_async_copy(cam_ref.at[index], tiles.at[c], sem.at[c]).start()

        for k, ref in ((1, r1_ref), (2, r2_ref), (3, r3_ref)):

            @pl.when(dist == k)
            def _():
                pltpu.make_async_copy(ref, tiles.at[c], sem.at[c]).start()

    for c in range(2):
        pltpu.make_async_copy(cam_ref.at[0], tiles.at[c], sem.at[c]).wait()
        for j in range(2):
            interp[2 * c + j] = jnp.dot(mats_ref[c], tiles[c, j], preferred_element_type=F32)

    rows = 32

    def cell_rows(step, _):
        q = pl.ds(pl.multiple_of(step * rows, rows), rows)
        parts = [interp[i, q, :] for i in range(4)]
        for k in range(3):
            total = coef_ref[q, 4 * k : 4 * k + 1] * parts[0]
            for i in range(1, 4):
                total = total + coef_ref[q, 4 * k + i : 4 * k + i + 1] * parts[i]
            vel_ref[0, k, q, :] = total.astype(BF16)
        return 0

    lax.fori_loop(0, cells // rows, cell_rows, 0)
    flat = vel_ref[0].reshape(3 * cells, snaps)
    for i in range(snaps // 256):
        left = flat[:, 256 * i : 256 * (i + 1)]
        block = lax.dot_general(left, flat[:, 256 * i :], (((0,), (0,)), ((), ())), preferred_element_type=F32)
        for j in range(2 * i, snaps // 128):
            part = block[:, 128 * j - 256 * i : 128 * (j + 1) - 256 * i]
            where = (j, pl.ds(256 * i, 256))
            if w:
                part = part + gin_ref[where]
            gram_ref[where] = part
        if i:
            for j in range(2 * i):
                gram_ref[j, pl.ds(256 * i, 256)] = jnp.zeros((256, 128), F32)


def world(w, pick, cam, recv, mats, coef, carry):
    snaps, cells = cam.shape[-1], mats.shape[1]
    world_tiles = 2
    in_specs = [pl.BlockSpec(memory_space=pltpu.SMEM)] + [ANY] * 4 + [VM, VM]
    args = [pick, cam, *recv, mats, coef]
    aliases = {}
    if w:
        in_specs += [VM, ANY]
        args += [carry[1], carry[0]]
        aliases = {len(args) - 1: 0}
    return pl.pallas_call(
        functools.partial(world_kernel, w),
        grid=(1,),
        in_specs=in_specs,
        out_specs=(
            pl.BlockSpec((1, 3, cells, snaps), lambda _: (w, 0, 0, 0)),
            pl.BlockSpec((snaps // 128, snaps, 128), lambda _: (0, 0, 0)),
        ),
        out_shape=(
            jax.ShapeDtypeStruct((world_tiles, 3, cells, snaps), BF16),
            jax.ShapeDtypeStruct((snaps // 128, snaps, 128), F32),
        ),
        scratch_shapes=[
            pltpu.VMEM((2, 2, cam.shape[2], snaps), BF16),
            pltpu.VMEM((4, cells, snaps), F32),
            pltpu.SemaphoreType.DMA((2,)),
        ],
        input_output_aliases=aliases,
        compiler_params=pltpu.CompilerParams(vmem_limit_bytes=32 << 20),
        cost_estimate=pl.CostEstimate(flops=700_000_000, bytes_accessed=4_000_000, transcendentals=0),
        name=f"world{w}",
    )(*args)


def inverse_factor(blocks):
    n, width = len(blocks), blocks[0].shape[1]
    lane = lax.broadcasted_iota(jnp.int32, (8, width), 1)
    sub = lax.broadcasted_iota(jnp.int32, (8, width), 0)
    slabs, out = list(blocks), []
    for s in range(n):
        k0 = 8 * s
        a = slabs[s]
        columns = [jnp.broadcast_to(a[:, k0 + j : k0 + j + 1], (8, width)) for j in range(8)]
        c = [[None] * 8 for _ in range(8)]
        for j in range(8):
            for i in range(j + 1):
                c[i][j] = jnp.broadcast_to(columns[j][i : i + 1, :], (8, width))
                c[j][i] = c[i][j]
        inside = (lane >= k0) & (lane < k0 + 8)
        aug = jnp.where(inside, jnp.where(lane - k0 == sub, 1.0, 0.0), a)
        r = [jnp.broadcast_to(aug[i : i + 1, :], (8, width)) for i in range(8)]
        scaled = [None] * 8
        for k in range(8):
            root = lax.rsqrt(c[k][k])
            inverse = root * root
            scaled[k] = r[k] * root
            t = r[k] * inverse
            ct = [None if j <= k else c[k][j] * inverse for j in range(8)]
            new = [row[:] for row in c]
            for i in range(8):
                if i == k:
                    continue
                r[i] = r[i] - c[i][k] * t
                for j in range(k + 1, 8):
                    if k < j < i:
                        continue
                    new[i][j] = c[i][j] - c[i][k] * ct[j]
                    if i > k:
                        new[j][i] = new[i][j]
            for j in range(k + 1, 8):
                new[k][j] = ct[j]
            c = new
            r[k] = t
        slab = scaled[7]
        for k in range(6, -1, -1):
            slab = jnp.where(sub == k, scaled[k], slab)
        out.append(jnp.where(lane < k0 + 8, slab, 0.0))
        for b in range(s + 1, n):
            x = slabs[b]
            total = jnp.where(inside, 0.0, x)
            for k in range(8):
                total = total - jnp.broadcast_to(x[:, k0 + k : k0 + k + 1], (8, width)) * r[k]
            slabs[b] = total
    return out


def exact_dot(a, b, dims):
    return lax.dot_general(a, b, ((dims[:1], dims[1:]), ((), ())), precision=lax.Precision.HIGHEST, preferred_element_type=F32)


def factor_kernel(g_ref, o_ref, s_ref):
    parts, size = g_ref.shape[0], 128
    n = parts * size
    for j in range(parts):
        s_ref[:, j * size : (j + 1) * size] = g_ref[j]
    o_ref[...] = jnp.zeros_like(o_ref)

    def panel(p, _):
        off = pl.multiple_of(p * size, size)
        blocks = [s_ref[pl.ds(off + 8 * i, 8), pl.ds(off, size)] for i in range(size // 8)]
        linv = jnp.concatenate(inverse_factor(blocks), axis=0)
        for q in range(parts):

            @pl.when(p == q)
            def _():
                lo, wide = q * size, n - q * size
                r = exact_dot(linv, s_ref[lo : lo + size, lo:], (1, 0))
                row = lax.broadcasted_iota(jnp.int32, (size, wide), 0)
                col = lax.broadcasted_iota(jnp.int32, (size, wide), 1)
                r = jnp.where(col >= row, r, 0.0)
                o_ref[lo : lo + size, lo:] = r
                if q < parts - 1:
                    t = r[:, size:]
                    s_ref[lo + size :, lo + size :] = s_ref[lo + size :, lo + size :] - exact_dot(t, t, (0, 0))

        return 0

    lax.fori_loop(0, parts, panel, 0)


def factor(gram):
    n = gram.shape[1]
    return pl.pallas_call(
        factor_kernel,
        out_shape=jax.ShapeDtypeStruct((n, n), F32),
        in_specs=[VM],
        out_specs=VM,
        scratch_shapes=[pltpu.VMEM((n, n), F32)],
        name="factor",
    )(gram)


def sum_devices(gram, scale):
    chips = lax.axis_size("y") * lax.axis_size("z") * lax.axis_size("x")
    flat = gram.reshape(2, -1, 128)
    half = flat.shape[1]
    core = lax.axis_index("core")
    swap = [(0, 1), (1, 0)]
    mine = lax.dynamic_index_in_dim(flat, core, 0, keepdims=False)
    other = lax.dynamic_index_in_dim(flat, 1 - core, 0, keepdims=False)
    mine = mine + lax.ppermute(other, "core", swap)
    pieces = lax.all_to_all(mine.reshape(chips, half // chips, 128), CHIPS, 0, 0)
    piece = jnp.sum(pieces, axis=0) * scale
    whole = lax.all_to_all(jnp.broadcast_to(piece, pieces.shape), CHIPS, 0, 0).reshape(half, 128)
    other = lax.ppermute(whole, "core", swap)
    first = core == 0
    both = jnp.stack([jnp.where(first, whole, other), jnp.where(first, other, whole)])
    return both.reshape(gram.shape)


def local(cam_disp, footprint, stencil, frac, coef):
    cam_count, pix, snaps = cam_disp.shape[2], cam_disp.shape[4], cam_disp.shape[5]
    world_tiles = footprint.shape[2]
    cells = coef.shape[-1]
    groups = lax.axis_size("x")
    me = lax.axis_index("x")
    tiles = cam_disp.reshape(cam_count, 2, pix, snaps)
    ids = footprint.reshape(world_tiles, 2)

    swaps = [[(i, i ^ k) for i in range(groups)] for k in range(groups)]
    asked = [None] + [lax.ppermute(ids, "x", swaps[k]) for k in range(1, groups)]
    received = []
    for w in range(world_tiles):
        got = []
        for k in range(1, groups):
            want = asked[k][w]
            index = jnp.where(want[0] // cam_count == me, want[0], want[1]) % cam_count
            got.append(lax.ppermute(lax.dynamic_index_in_dim(tiles, index, 0, keepdims=False), "x", swaps[k]))
        received.append(got)

    sten = stencil.reshape(world_tiles * 2, 2, cells)
    fraction = frac.reshape(world_tiles * 2, 2, cells)
    row_weights = axis_weights(sten[:, 0], fraction[:, 0], TILE_SIDE)
    col_weights = axis_weights(sten[:, 1], fraction[:, 1], TILE_SIDE)
    mats = (row_weights[:, :, :, None] * col_weights[:, :, None, :]).reshape(world_tiles, 2, cells, pix).astype(BF16)
    coef_cells = coef.reshape(world_tiles, 12, cells).transpose(0, 2, 1)
    pick = jnp.stack([(ids // cam_count) ^ me, ids % cam_count], axis=-1).reshape(-1)

    carry = None
    for w in range(world_tiles):
        carry = world(w, pick, tiles, received[w], mats[w], coef_cells[w], carry)
    velocity, gram = carry
    total_rows = groups * lax.axis_size("y") * lax.axis_size("z") * 2 * world_tiles * 3 * cells
    gram = sum_devices(gram, F32(1.0 / total_rows))
    return (velocity.reshape(1, 1, world_tiles, 3, cells, snaps), factor(gram))


def solution(mesh):
    grid = Mesh(mesh.devices.reshape(4, 4, 2, 4), ("y", "z", "core", "x"))
    columns = ("y", "z", "core")
    in_specs = (
        P("x", columns, None, None, None, None),
        P("x", columns, None, None),
        P("x", columns, None, None, None, None),
        P("x", columns, None, None, None, None),
        P("x", columns, None, None, None, None),
    )
    out_specs = (P("x", columns, None, None, None, None), P())
    return jax.shard_map(local, mesh=grid, in_specs=in_specs, out_specs=out_specs, check_vma=False)
```

time: 351 us -> 161 us (0.46)
  waiting for transfers between devices: 226 us -> 37.3 us
  other arithmetic: 84 us -> 1.5 us
  blocking collectives: 0 us -> 36.7 us
  Pallas kernels: 0 us -> 31.3 us
  starting transfers between devices: 0.08 us -> 19.9 us
  local copies, waits for them, and re-layouts: 17.6 us -> 9.3 us
  between operations: 16.9 us -> 24.3 us
  matrix products: 6.25 us -> 0 us
    psum x1 -> x0, waiting for transfers between devices: 142 us -> none  [local(): gram = lax.psum(gram_local, ('tile', 'row'))]
    all_gather x1 -> x0, waiting for transfers between devices: 83.4 us -> none  [local(): pool = lax.all_gather(tiles, 'row', axis=0, tiled=True)]
    another operation x15 -> x3, other arithmetic: 79.3 us -> 1.16 us  [the longest x2 1.16 us: sum_devices(): jnp.stack([jnp.where(first, whole, other), jnp.where(first, other, whole)])]
    ppermute x0 -> x11, waiting for transfers between devices: none -> 37.3 us  [the longest x6 34.2 us: local(): lax.ppermute(lax.dynamic_index_in_dim(tiles, index, 0, keepdims=False), '...]
    all_to_all x0 -> x2, blocking collectives: none -> 36.7 us  [the longest x1 21.2 us: sum_devices(): lax.all_to_all(mine.reshape(chips, half // chips, 128), CHIPS, 0, 0)]
    pallas_call x0 -> x3, Pallas kernels: none -> 31.3 us  [the longest x1 22.7 us: factor(): pl.pallas_call(factor_kernel, out_shape=jax.ShapeDtypeStruct((n, n), F32)...]
    ppermute x0 -> x11, starting transfers between devices: none -> 19.9 us  [the longest x6 9.23 us: local(): lax.ppermute(lax.dynamic_index_in_dim(tiles, index, 0, keepdims=False), '...]
    mul x11 -> x0, local copies, waits for them, and re-layouts: 5.22 us -> none  [local(): total = total + weights_coef[:, :, inner, :, None] * interp[:, None, inner]]
  transfers between devices with their start and end apart: 2 -> 11, of which waited for: 2 -> 8; matrix products, arithmetic and copies ran while one was open for 3% -> 3% of each run, Pallas kernels for 0% -> 3%
where the time goes in v1:
time: 161 us; the launch traced here: 160 us
  waiting for transfers between devices  37.3 us (23%)
  blocking collectives  36.7 us (23%)
  Pallas kernels  31.3 us (19%)
  between operations  24.3 us (15%)
  starting transfers between devices  19.9 us (12%)
  local copies, waits for them, and re-layouts  9.3 us (6%)
    ppermute x6, waiting for transfers between devices, local(): lax.ppermute(lax.dynamic_index_in_dim(tiles, index, 0, keepdims=False), '...  34.2 us
    pallas_call x1, Pallas kernels, factor(): pl.pallas_call(factor_kernel, out_shape=jax.ShapeDtypeStruct((n, n), F32)...  22.7 us
    all_to_all x1, blocking collectives, sum_devices(): lax.all_to_all(mine.reshape(chips, half // chips, 128), CHIPS, 0, 0)  21.2 us
    all_to_all x1, blocking collectives, sum_devices(): lax.all_to_all(jnp.broadcast_to(piece, pieces.shape), CHIPS, 0, 0)  15.5 us
    ppermute x6, starting transfers between devices, local(): lax.ppermute(lax.dynamic_index_in_dim(tiles, index, 0, keepdims=False), '...  9.23 us
    pallas_call x2, Pallas kernels, world(): pl.pallas_call(functools.partial(world_kernel, w), grid=(1,), in_specs=in...  8.61 us
    ppermute x3, starting transfers between devices, local(): lax.ppermute(ids, 'x', swaps[k])  4.5 us
    squeeze x1, local copies, waits for them, and re-layouts, local(): lax.dynamic_index_in_dim(tiles, index, 0, keepdims=False)  3.36 us
  transfers between devices with their start and end apart: 11, of which 8 were waited for; matrix products, arithmetic and copies ran while one was open for 3% of the time, Pallas kernels for 3%

profile of v1, /device:TPU:1, one launch (start us, length us, event | category | flops | bytes accessed | tf_op | source)
XLA Modules:
  0.0 160.3 jit_solution(10706199691796802138)
XLA Ops:
  0.6 3.6 %collective-permute-start.2 = (s32[2,2]{1,0:T(2,128)}, s32[2,2]{1,0:T(2,128)S(1)}, u32[]{:S(2)}, u32[]{:S(2)}) collective-permute-start(s32[2,2]{1,0:T(2,128)} %bitcast.148), channel_id=1, source_target_pairs={{0,2},{1,3},{2,0},{3,1},{4,6},{5,7},{6,4},{7,5},{8,10},{9,11},{10,... | collective-permute-start | bytes 56 | tf_op jit(solution)/shard_map/ppermute | solution.py:248
  4.3 0.3 collective-permute-start
  4.6 0.6 collective-permute-start.4
  5.1 0.8 fusion.10
  5.9 0.8 fusion.11
  6.8 0.0 collective-permute-done.2
  6.8 0.7 fusion.13
  11.4 0.0 collective-permute-done
  11.4 0.6 fusion.14
  19.8 0.0 collective-permute-done.4
  19.8 0.7 fusion.12
  32.3 0.0 copy-start.2
  32.3 3.4 %dynamic-slice_bitcast_fusion.1 = (bf16[2,256,512]{2,1,0:T(8,128)(2,1)}, bf16[2,256,512]{2,1,0:T(8,128)(2,1)S(1)}, bf16[2,256,512]{2,1,0:T(8,128)(2,1)}, bf16[2,...) fusion(bf16[1,1,4,2,256,512]{5,4,3,2,1,0:T(8,128)(2,1)} %param.5, ...), kind=kLoop, calls=%fused_computation.6 | loop fusion | bytes 6291480 | tf_op jit(solution)/shard_map/jit(dynamic_index_in_dim)/squeeze | solution.py:255
  35.6 0.0 copy-start.1
  35.6 0.0 copy-start
  35.6 1.0 collective-permute-start.6
  36.6 0.1 multiply_convert_fusion
  36.8 2.5 %collective-permute-start.7 = (bf16[2,256,512]{2,1,0:T(8,128)(2,1)}, bf16[2,256,512]{2,1,0:T(8,128)(2,1)}, u32[]{:S(2)}, u32[]{:S(2)}) collective-permute-start(bf16[2,256,512]{2,1,0:T(8,128)(2,1)} %get-tuple-element.15), channel_id=1, source_target_pairs={{0,2},{1,3},{2,0},{3,1},{4,6},{5,7},{6,4},{7,5},{8,10},{9,11},{10,... | collective-permute-start | bytes 1572872 | tf_op jit(solution)/shard_map/ppermute | solution.py:255
  39.3 0.5 collective-permute-start.8
  39.8 0.0 collective-permute-start.1
  39.8 3.3 %collective-permute-start.3 = (bf16[2,256,512]{2,1,0:T(8,128)(2,1)}, bf16[2,256,512]{2,1,0:T(8,128)(2,1)}, u32[]{:S(2)}, u32[]{:S(2)}) collective-permute-start(bf16[2,256,512]{2,1,0:T(8,128)(2,1)} %get-tuple-element.13), channel_id=1, source_target_pairs={{0,2},{1,3},{2,0},{3,1},{4,6},{5,7},{6,4},{7,5},{8,10},{9,11},{10,... | collective-permute-start | bytes 1572872 | tf_op jit(solution)/shard_map/ppermute | solution.py:255
  43.2 4.9 %collective-permute-done.6.r1_ref = bf16[2,256,512]{2,1,0:T(8,128)(2,1)S(1)} collective-permute-done((bf16[2,256,512]{2,1,0:T(8,128)(2,1)S(1)}, bf16[2,256,512]{2,1,0:T(8,128)(2,1)S(1)}, u32[]{:S(2)}, u32[]{:S(2)}) %collective-permute-start.6) | collective-permute-done | bytes 524320 | tf_op jit(solution)/shard_map/ppermute | solution.py:255
  48.0 1.9 %collective-permute-start.5 = (bf16[2,256,512]{2,1,0:T(8,128)(2,1)}, bf16[2,256,512]{2,1,0:T(8,128)(2,1)}, u32[]{:S(2)}, u32[]{:S(2)}) collective-permute-start(bf16[2,256,512]{2,1,0:T(8,128)(2,1)} %get-tuple-element.12), channel_id=1, source_target_pairs={{0,3},{1,2},{2,1},{3,0},{4,7},{5,6},{6,5},{7,4},{8,11},{9,10},{10,... | collective-permute-start | bytes 1572872 | tf_op jit(solution)/shard_map/ppermute | solution.py:255
  49.9 0.0 copy-done.2
  50.0 0.1 copy.17.mats_ref
  50.1 0.1 copy.12
  50.2 0.1 reshape.390.pick_ref
  50.3 0.0 copy-done.1
  50.3 0.9 copy.16
  51.2 0.1 copy.18.mats_ref
  51.3 1.0 slice_bitcast_fusion
  52.3 8.6 %collective-permute-done.7.r2_ref = bf16[2,256,512]{2,1,0:T(8,128)(2,1)} collective-permute-done((bf16[2,256,512]{2,1,0:T(8,128)(2,1)}, bf16[2,256,512]{2,1,0:T(8,128)(2,1)}, u32[]{:S(2)}, u32[]{:S(2)}) %collective-permute-start.7) | collective-permute-done | bytes 524320 | tf_op jit(solution)/shard_map/ppermute | solution.py:255
  60.9 1.2 collective-permute-done.8.r3_ref
  62.2 0.0 copy-done
  62.2 4.3 %world0.1 = (bf16[2,3,256,512]{3,2,1,0:T(8,128)(2,1)}, f32[4,512,128]{2,1,0:T(8,128)S(1)}) custom-call(s32[8]{0:T(128)S(1)} %reshape.390.pick_ref, bf16[4,2,256,512]{3,2,1,0:T(8,128)(2,1)S(1)} %bitcast.134, bf16[2,256,512]{2,1,0:T(8,128)(2,1)S(1)} %collective-permute-done.6.r1_ref, bf16[2,256,512]{2,1,0:T(8,128)(2,1)} %collective-permute-done.7.r2_ref, ...), custom_call_target="tpu_custom_call" | custom-call | flops 700000000 | bytes 4000000 | tf_op jit(solution)/shard_map/world0/pallas_call | solution.py:98
  66.5 4.0 %collective-permute-done.1.r1_ref = bf16[2,256,512]{2,1,0:T(8,128)(2,1)} collective-permute-done((bf16[2,256,512]{2,1,0:T(8,128)(2,1)}, bf16[2,256,512]{2,1,0:T(8,128)(2,1)}, u32[]{:S(2)}, u32[]{:S(2)}) %collective-permute-start.1) | collective-permute-done | bytes 524320 | tf_op jit(solution)/shard_map/ppermute | solution.py:255
  70.5 12.9 %collective-permute-done.3.r2_ref = bf16[2,256,512]{2,1,0:T(8,128)(2,1)} collective-permute-done((bf16[2,256,512]{2,1,0:T(8,128)(2,1)}, bf16[2,256,512]{2,1,0:T(8,128)(2,1)}, u32[]{:S(2)}, u32[]{:S(2)}) %collective-permute-start.3) | collective-permute-done | bytes 524320 | tf_op jit(solution)/shard_map/ppermute | solution.py:255
  83.5 2.5 %collective-permute-done.5.r3_ref = bf16[2,256,512]{2,1,0:T(8,128)(2,1)} collective-permute-done((bf16[2,256,512]{2,1,0:T(8,128)(2,1)}, bf16[2,256,512]{2,1,0:T(8,128)(2,1)}, u32[]{:S(2)}, u32[]{:S(2)}) %collective-permute-start.5) | collective-permute-done | bytes 524320 | tf_op jit(solution)/shard_map/ppermute | solution.py:255
  86.0 4.3 %world1.1 = (bf16[2,3,256,512]{3,2,1,0:T(8,128)(2,1)}, f32[4,512,128]{2,1,0:T(8,128)S(1)}) custom-call(s32[8]{0:T(128)S(1)} %reshape.390.pick_ref, bf16[4,2,256,512]{3,2,1,0:T(8,128)(2,1)S(1)} %bitcast.135, bf16[2,256,512]{2,1,0:T(8,128)(2,1)} %collective-permute-done.1.r1_ref, ...), custom_call_target="tpu_custom_call", output_to_operand_aliasing={{0}: (8, {})} | custom-call | flops 700000000 | bytes 4000000 | tf_op jit(solution)/shard_map/world1/pallas_call | solution.py:98
  90.3 3.0 %collective-permute-start.9 = (f32[1024,128]{1,0:T(8,128)S(1)}, f32[1024,128]{1,0:T(8,128)S(1)}, u32[]{:S(2)}, u32[]{:S(2)}) collective-permute-start(f32[1024,128]{1,0:T(8,128)S(1)} %dynamic-slice_bitcast_fusion), channel_id=1, source_target_pairs={{0,4},{4,0},{1,5},{5,1},{2,6},{6,2},{3,7},{7,3},{8,12},{12,8},{9,1... | collective-permute-start | bytes 1572872 | tf_op jit(solution)/shard_map/ppermute | solution.py:228
  93.3 1.5 collective-permute-done.9
  94.9 0.1 bitcast_add_fusion
  94.9 21.2 %all_to_all.10 = f32[64,16,128]{2,1,0:T(8,128)S(1)} all-to-all(f32[64,16,128]{2,1,0:T(8,128)S(1)} %bitcast.140), channel_id=1, replica_groups=mesh['y'=4,'z'=4,'core'=2,'x'=4] {'y','z','x'}, dimensions={0} | all-to-all | bytes 1048576 | tf_op jit(solution)/shard_map/all_to_all | solution.py:229
  116.1 0.1 reduce_sum.9
  116.2 15.5 %all_to_all.11 = f32[64,16,128]{2,1,0:T(8,128)S(1)} all-to-all(f32[64,16,128]{2,1,0:T(8,128)S(1)} %broadcast_in_dim.2), channel_id=1, replica_groups=mesh['y'=4,'z'=4,'core'=2,'x'=4] {'y','z','x'}, dimensions={0} | all-to-all | bytes 1048576 | tf_op jit(solution)/shard_map/all_to_all | solution.py:231
  131.8 3.1 %collective-permute-start.10 = (f32[1024,128]{1,0:T(8,128)S(1)}, f32[1024,128]{1,0:T(8,128)S(1)}, u32[]{:S(2)}, u32[]{:S(2)}) collective-permute-start(f32[1024,128]{1,0:T(8,128)S(1)} %bitcast.139), channel_id=1, source_target_pairs={{0,4},{4,0},{1,5},{5,1},{2,6},{6,2},{3,7},{7,3},{8,12},{12,8},{9,1... | collective-permute-start | bytes 1572872 | tf_op jit(solution)/shard_map/ppermute | solution.py:232
  134.9 1.5 collective-permute-done.10
  136.5 0.1 select_bitcast_fusion.1
  136.5 1.1 pad_maximum_fusion
  137.6 22.7 %factor.1 = f32[512,512]{1,0:T(8,128)} custom-call(f32[4,512,128]{2,1,0:T(8,128)} %bitcast.138), custom_call_target="tpu_custom_call" | custom-call | tf_op jit(solution)/shard_map/factor/pallas_call | solution.py:210
  (12 shorter events, 0.2 us)
Async XLA Ops:
  0.6 6.2 %collective-permute-start.2 = (s32[2,2]{1,0:T(2,128)}, s32[2,2]{1,0:T(2,128)S(1)}, u32[]{:S(2)}, u32[]{:S(2)}) collective-permute-start(s32[2,2]{1,0:T(2,128)} %bitcast.148), channel_id=1, source_target_pairs={{0,2},{1,3},{2,0},{3,1},{4,6},{5,7},{6,4},{7,5},{8,10},{9,11},{10,... | collective-permute-start | bytes 56 | tf_op jit(solution)/shard_map/ppermute | solution.py:248
  4.3 7.1 %collective-permute-start = (s32[2,2]{1,0:T(2,128)}, s32[2,2]{1,0:T(2,128)S(1)}, u32[]{:S(2)}, u32[]{:S(2)}) collective-permute-start(s32[2,2]{1,0:T(2,128)} %bitcast.149), channel_id=1, source_target_pairs={{0,1},{1,0},{2,3},{3,2},{4,5},{5,4},{6,7},{7,6},{8,9},{9,8},{10,11... | collective-permute-start | bytes 56 | tf_op jit(solution)/shard_map/ppermute | solution.py:248
  4.6 15.2 %collective-permute-start.4 = (s32[2,2]{1,0:T(2,128)}, s32[2,2]{1,0:T(2,128)S(1)}, u32[]{:S(2)}, u32[]{:S(2)}) collective-permute-start(s32[2,2]{1,0:T(2,128)} %bitcast.150), channel_id=1, source_target_pairs={{0,3},{1,2},{2,1},{3,0},{4,7},{5,6},{6,5},{7,4},{8,11},{9,10},{10,... | collective-permute-start | bytes 56 | tf_op jit(solution)/shard_map/ppermute | solution.py:248
  32.3 17.7 %copy-start.2 = (s32[1,1,2,2]{3,2,1,0:T(2,128)S(1)}, s32[1,1,2,2]{3,2,1,0:T(2,128)}, u32[]{:S(2)}) copy-start(s32[1,1,2,2]{3,2,1,0:T(2,128)} %param.6) | copy-start | bytes 52
  35.6 14.7 %copy-start.1 = (f32[1,1,2,3,4,256]{5,4,3,2,1,0:T(4,128)S(1)}, f32[1,1,2,3,4,256]{5,4,3,2,1,0:T(4,128)}, u32[]{:S(2)}) copy-start(f32[1,1,2,3,4,256]{5,4,3,2,1,0:T(4,128)} %param.9) | copy-start | bytes 73732
  35.6 26.5 %copy-start = (bf16[1,1,4,2,256,512]{5,4,3,2,1,0:T(8,128)(2,1)S(1)}, bf16[1,1,4,2,256,512]{5,4,3,2,1,0:T(8,128)(2,1)}, u32[]{:S(2)}) copy-start(bf16[1,1,4,2,256,512]{5,4,3,2,1,0:T(8,128)(2,1)} %param.5) | copy-start | bytes 6291460
  35.6 12.4 %collective-permute-start.6 = (bf16[2,256,512]{2,1,0:T(8,128)(2,1)S(1)}, bf16[2,256,512]{2,1,0:T(8,128)(2,1)S(1)}, u32[]{:S(2)}, u32[]{:S(2)}) collective-permute-start(bf16[2,256,512]{2,1,0:T(8,128)(2,1)S(1)} %get-tuple-element.11), channel_id=1, source_target_pairs={{0,1},{1,0},{2,3},{3,2},{4,5},{5,4},{6,7},{7,6},{8,9},{9,8},{10,11... | collective-permute-start | bytes 1572872 | tf_op jit(solution)/shard_map/ppermute | solution.py:255
  36.8 24.1 %collective-permute-start.7 = (bf16[2,256,512]{2,1,0:T(8,128)(2,1)}, bf16[2,256,512]{2,1,0:T(8,128)(2,1)}, u32[]{:S(2)}, u32[]{:S(2)}) collective-permute-start(bf16[2,256,512]{2,1,0:T(8,128)(2,1)} %get-tuple-element.15), channel_id=1, source_target_pairs={{0,2},{1,3},{2,0},{3,1},{4,6},{5,7},{6,4},{7,5},{8,10},{9,11},{10,... | collective-permute-start | bytes 1572872 | tf_op jit(solution)/shard_map/ppermute | solution.py:255
  39.3 22.9 %collective-permute-start.8 = (bf16[2,256,512]{2,1,0:T(8,128)(2,1)}, bf16[2,256,512]{2,1,0:T(8,128)(2,1)}, u32[]{:S(2)}, u32[]{:S(2)}) collective-permute-start(bf16[2,256,512]{2,1,0:T(8,128)(2,1)} %get-tuple-element.10), channel_id=1, source_target_pairs={{0,3},{1,2},{2,1},{3,0},{4,7},{5,6},{6,5},{7,4},{8,11},{9,10},{10,... | collective-permute-start | bytes 1572872 | tf_op jit(solution)/shard_map/ppermute | solution.py:255
  39.8 30.7 %collective-permute-start.1 = (bf16[2,256,512]{2,1,0:T(8,128)(2,1)}, bf16[2,256,512]{2,1,0:T(8,128)(2,1)}, u32[]{:S(2)}, u32[]{:S(2)}) collective-permute-start(bf16[2,256,512]{2,1,0:T(8,128)(2,1)} %get-tuple-element.14), channel_id=1, source_target_pairs={{0,1},{1,0},{2,3},{3,2},{4,5},{5,4},{6,7},{7,6},{8,9},{9,8},{10,11... | collective-permute-start | bytes 1572872 | tf_op jit(solution)/shard_map/ppermute | solution.py:255
  39.8 43.6 %collective-permute-start.3 = (bf16[2,256,512]{2,1,0:T(8,128)(2,1)}, bf16[2,256,512]{2,1,0:T(8,128)(2,1)}, u32[]{:S(2)}, u32[]{:S(2)}) collective-permute-start(bf16[2,256,512]{2,1,0:T(8,128)(2,1)} %get-tuple-element.13), channel_id=1, source_target_pairs={{0,2},{1,3},{2,0},{3,1},{4,6},{5,7},{6,4},{7,5},{8,10},{9,11},{10,... | collective-permute-start | bytes 1572872 | tf_op jit(solution)/shard_map/ppermute | solution.py:255
  48.0 37.9 %collective-permute-start.5 = (bf16[2,256,512]{2,1,0:T(8,128)(2,1)}, bf16[2,256,512]{2,1,0:T(8,128)(2,1)}, u32[]{:S(2)}, u32[]{:S(2)}) collective-permute-start(bf16[2,256,512]{2,1,0:T(8,128)(2,1)} %get-tuple-element.12), channel_id=1, source_target_pairs={{0,3},{1,2},{2,1},{3,0},{4,7},{5,6},{6,5},{7,4},{8,11},{9,10},{10,... | collective-permute-start | bytes 1572872 | tf_op jit(solution)/shard_map/ppermute | solution.py:255
  90.3 4.5 %collective-permute-start.9 = (f32[1024,128]{1,0:T(8,128)S(1)}, f32[1024,128]{1,0:T(8,128)S(1)}, u32[]{:S(2)}, u32[]{:S(2)}) collective-permute-start(f32[1024,128]{1,0:T(8,128)S(1)} %dynamic-slice_bitcast_fusion), channel_id=1, source_target_pairs={{0,4},{4,0},{1,5},{5,1},{2,6},{6,2},{3,7},{7,3},{8,12},{12,8},{9,1... | collective-permute-start | bytes 1572872 | tf_op jit(solution)/shard_map/ppermute | solution.py:228
  131.8 4.7 %collective-permute-start.10 = (f32[1024,128]{1,0:T(8,128)S(1)}, f32[1024,128]{1,0:T(8,128)S(1)}, u32[]{:S(2)}, u32[]{:S(2)}) collective-permute-start(f32[1024,128]{1,0:T(8,128)S(1)} %bitcast.139), channel_id=1, source_target_pairs={{0,4},{4,0},{1,5},{5,1},{2,6},{6,2},{3,7},{7,3},{8,12},{12,8},{9,1... | collective-permute-start | bytes 1572872 | tf_op jit(solution)/shard_map/ppermute | solution.py:232
